TPU v7x, 32 devices: a whole 2x2x4 slice. The times are simulated.
32 devices in a mesh: parts: 1, seq: 32 (over z, y, x, core).
Axes of the slice: x: 2, y: 2, z: 4, core: 2. Of those that a mesh axis runs over, the one named last changes fastest.
Arguments:
- tokens: bfloat16 [1, 128, 3, 128, 3072], P('parts', 'seq'), may hold values from -6 to 6
- queries: bfloat16 [1, 128, 3, 128, 1536], P('parts', 'seq'), may hold values from -68 to 68
- key_weight: bfloat16 [3072, 1536], P('seq'), may hold values from -0.109375 to 0.109375
- value_weight: bfloat16 [3072, 1536], P('seq'), may hold values from -0.109375 to 0.109375
- halves: int32 [1, 128, 3, 2, 2], P('parts', 'seq'), may hold values from 1 to 3
Outputs:
- mixed: bfloat16 [1, 128, 3, 128, 1536], P('parts', 'seq')
Inputs may be any that keep to these rules, and one draw needn't show every extreme that they name: `halves`: 1 lists the first half of the partner lines, 2 the second half, 3 both.
All inputs are finite; a program needn't handle non-finite values.
Results may differ from a plain program's by a relative error of at most 0.012.
Values may be sent and summed in bfloat16 or wider, within the bound.
No kernel may reach another device: no remote copies, remote signals or barrier semaphores. Data moves between devices by JAX's collectives and lax.ppermute only.
A program may use at most 128 MiB of HBM per device.

v0:
```python
import math
import jax
import jax.numpy as jnp
from jax import lax
from jax.sharding import PartitionSpec as P

HEADS = 12
HDIM = 128


def split_heads(tensor_in):
    return tensor_in.reshape(tensor_in.shape[:-1] + (HEADS, HDIM))


def kept_keys(code_grid, grid_len):
    column = jnp.arange(grid_len)
    first_kept = (code_grid % 2 == 1)[..., None]
    second_kept = (code_grid >= 2)[..., None]
    return jnp.where(column < grid_len // 2, first_kept, second_kept)[..., None, :]


def codes_by_half(code_pairs, half_index):
    return jnp.where(half_index[None, None, :] == 0, code_pairs[..., 0:1], code_pairs[..., 1:2])


def partial_attention(queries_h, keys_h, values_h, score_form, value_form, kept_mask):
    scores = jnp.einsum(score_form, queries_h, keys_h, preferred_element_type=jnp.float32) * (
        1.0 / math.sqrt(HDIM)
    )
    masked = jnp.where(kept_mask, scores, -jnp.inf)
    peak_val = jnp.max(masked, axis=-1)
    weights = jnp.exp(masked - peak_val[..., None])
    totals = jnp.sum(weights, axis=-1)
    partial_out = jnp.einsum(
        value_form, weights.astype(jnp.bfloat16), values_h, preferred_element_type=jnp.float32
    )
    return (partial_out, peak_val, totals)


def merge_slots(near_part, far_part):
    peak_val = jnp.maximum(near_part[1], far_part[1])
    near_w = jnp.exp(near_part[1] - peak_val)
    far_w = jnp.exp(far_part[1] - peak_val) * far_part[2]
    upper = near_part[0] * near_w[..., None] + far_part[0] * far_w[..., None]
    return upper / (near_part[2] * near_w + far_w)[..., None]


def on_device(tokens, queries, key_weight, value_weight, halves):
    scenes, line_count, planes, grid_len, model_width = tokens.shape
    hidden_width = queries.shape[-1]
    home_rows = tokens.reshape(-1, model_width)

    def add_panel(weight_panel):
        return jnp.dot(home_rows, weight_panel, preferred_element_type=jnp.float32)

    key_sum = add_panel(lax.all_gather(key_weight, "seq", axis=0, tiled=True))
    value_sum = add_panel(lax.all_gather(value_weight, "seq", axis=0, tiled=True))
    home_shape = (scenes, line_count, planes, grid_len, hidden_width)
    keys_home = key_sum.astype(jnp.bfloat16).reshape(home_shape)
    values_home = value_sum.astype(jnp.bfloat16).reshape(home_shape)
    moved_q, moved_k, moved_v = (
        lax.all_to_all(queries, "seq", split_axis=3, concat_axis=1, tiled=True),
        lax.all_to_all(keys_home, "seq", split_axis=3, concat_axis=1, tiled=True),
        lax.all_to_all(values_home, "seq", split_axis=3, concat_axis=1, tiled=True),
    )
    code_table = lax.all_gather(halves, "seq", axis=1, tiled=True)
    half_len = grid_len // 2
    own_start = lax.axis_index("seq") * line_count
    moved_half = (own_start + jnp.arange(line_count)) // half_len
    home_half = jnp.arange(grid_len) // half_len
    remote_plan = (
        (0, keys_home[:, :, 2], values_home[:, :, 2], "sabhd,sbjhd->sabhj", "sabhj,sbjhd->sabhd"),
        (1, moved_k[:, :, 2], moved_v[:, :, 2], "sabhd,sjbhd->sabhj", "sabhj,sjbhd->sabhd"),
        (2, moved_k[:, :, 1], moved_v[:, :, 1], "sabhd,sjbhd->sabhj", "sabhj,sjbhd->sabhd"),
    )
    remote_results = []
    for plane_idx, keys_part, values_part, score_form, value_form in remote_plan:
        code_grid = codes_by_half(code_table[:, :, plane_idx, :, 1], moved_half)
        remote_results.append(
            partial_attention(
                split_heads(moved_q[:, :, plane_idx]),
                split_heads(keys_part),
                split_heads(values_part),
                score_form,
                value_form,
                kept_keys(code_grid, grid_len),
            )
        )
    remote_mean = jnp.stack([result[0] / result[2][..., None] for result in remote_results], axis=2)
    remote_mean = remote_mean.reshape(remote_mean.shape[:4] + (hidden_width,)).astype(jnp.bfloat16)
    remote_peak = jnp.stack([result[1] for result in remote_results], axis=2)
    remote_sum = jnp.stack([result[2] for result in remote_results], axis=2)
    back_mean = lax.all_to_all(remote_mean, "seq", split_axis=1, concat_axis=3, tiled=True)
    back_peak, back_sum = (
        lax.all_to_all(remote_peak, "seq", split_axis=1, concat_axis=3, tiled=True),
        lax.all_to_all(remote_sum, "seq", split_axis=1, concat_axis=3, tiled=True),
    )
    home_plan = (
        (0, keys_home[:, :, 1], values_home[:, :, 1], "sabhd,sajhd->sabhj", "sabhj,sajhd->sabhd"),
        (1, keys_home[:, :, 0], values_home[:, :, 0], "sabhd,sajhd->sabhj", "sabhj,sajhd->sabhd"),
        (2, moved_k[:, :, 0], moved_v[:, :, 0], "sabhd,sjahd->sabhj", "sabhj,sjahd->sabhd"),
    )
    home_results = []
    for plane_idx, keys_part, values_part, score_form, value_form in home_plan:
        code_grid = codes_by_half(halves[:, :, plane_idx, :, 0], home_half)
        home_results.append(
            partial_attention(
                split_heads(queries[:, :, plane_idx]),
                split_heads(keys_part),
                split_heads(values_part),
                score_form,
                value_form,
                kept_keys(code_grid, grid_len),
            )
        )
    home_out = jnp.stack([result[0] for result in home_results], axis=2)
    home_peak = jnp.stack([result[1] for result in home_results], axis=2)
    home_sum = jnp.stack([result[2] for result in home_results], axis=2)
    merged = merge_slots(
        (home_out, home_peak, home_sum),
        (split_heads(back_mean.astype(jnp.float32)), back_peak, back_sum),
    )
    return merged.reshape(home_shape).astype(jnp.bfloat16)


def solution(mesh):
    in_specs = (
        P("parts", "seq", None, None, None),
        P("parts", "seq", None, None, None),
        P("seq", None),
        P("seq", None),
        P("parts", "seq", None, None, None),
    )
    out_specs = P("parts", "seq", None, None, None)
    return jax.shard_map(
        on_device, mesh=mesh, in_specs=in_specs, out_specs=out_specs, check_vma=False
    )
```

profile of v0, /device:TPU:0, one launch (start us, length us, event | category | flops | bytes accessed | tf_op | source)
XLA Modules:
  0.0 732.5 jit_solution(9357103538851799629)
XLA Ops:
  8.0 8.2 %copy.418 = bf16[1,4,3,128,1536]{4,1,2,0,3:T(4,128)(2,1)} copy(bf16[1,4,3,128,1536]{4,3,2,1,0:T(8,128)(2,1)} %param.6) | data formatting | bytes 9437184 | tf_op args[1]
  16.2 7.4 %all-to-all-start.2 = ((bf16[1,4,3,128,1536]{4,1,2,0,3:T(4,128)(2,1)}), bf16[1,4,3,128,1536]{4,1,2,0,3:T(4,128)(2,1)}, u32[]{:S(2)}, u32[]{:S(2)}) async-start(bf16[1,4,3,128,1536]{4,1,2,0,3:T(4,128)(2,1)} %copy.418), calls=%async_computation.2 | async-start | bytes 9437184 | tf_op jit(solution)/shard_map/all_to_all | solution.py:62
  23.6 128.7 %all-gather.3.cloned.1.call-done = bf16[3072,1536]{1,0:T(8,128)(2,1)} async-done(((bf16[96,1536]{1,0:T(8,128)(2,1)}), bf16[3072,1536]{1,0:T(8,128)(2,1)}) %all-gather.3.cloned.1.call-update) | async-done | bytes 9437200 | tf_op jit(solution)/shard_map/all_gather | solution.py:57
  152.3 19.9 %convolution_convert_fusion.1 = bf16[1536,1536]{1,0:T(8,128)(2,1)S(1)} fusion(bf16[1536,3072]{1,0:T(8,128)(2,1)} %bitcast.326, bf16[3072,1536]{1,0:T(8,128)(2,1)} %all-gather.3.cloned.1.call-done), kind=kOutput, calls=%fused_computation.7 | convolution fusion | flops 14497873920 | bytes 23592960 | tf_op jit(solution)/shard_map/dot_general | solution.py:54
  174.3 5.8 copy.400
  184.0 105.3 %all-gather.5.cloned.1.call-done = bf16[3072,1536]{1,0:T(8,128)(2,1)} async-done(((bf16[96,1536]{1,0:T(8,128)(2,1)}), bf16[3072,1536]{1,0:T(8,128)(2,1)}) %all-gather.5.cloned.1.call-update) | async-done | bytes 9437200 | tf_op jit(solution)/shard_map/all_gather | solution.py:56
  289.3 19.9 %convolution_convert_fusion = bf16[1536,1536]{1,0:T(8,128)(2,1)S(1)} fusion(bf16[1536,3072]{1,0:T(8,128)(2,1)} %bitcast.327, bf16[3072,1536]{1,0:T(8,128)(2,1)} %all-gather.5.cloned.1.call-done), kind=kOutput, calls=%fused_computation.6 | convolution fusion | flops 14497873920 | bytes 23592960 | tf_op jit(solution)/shard_map/dot_general | solution.py:54
  311.4 5.8 copy.404
  317.2 7.0 all-to-all-done
  328.1 113.8 %all_gather.11 = s32[1,128,3,2,2]{2,4,3,0,1:T(2,128)S(1)} all-gather(s32[1,4,3,2,2]{2,4,3,0,1:T(2,128)S(1)} %copy.415), channel_id=1, replica_groups=mesh['parts'=1,'seq'=32] {'seq'}, dimensions={1}, use_global_device_ids=true | all-gather | bytes 6336 | tf_op jit(solution)/shard_map/all_gather | solution.py:66
  443.1 4.7 copy.419
  459.9 4.4 fusion.97
  465.9 4.5 fusion.96
  519.5 19.8 %all-to-all-start.3 = ((f32[32,1,576]{2,1,0:T(1,128)}), f32[32,1,576]{2,1,0:T(1,128)S(1)}, u32[]{:S(2)}, u32[]{:S(2)}) async-start(f32[32,1,576]{2,1,0:T(1,128)} %reshape.1497), calls=%async_computation.3 | async-start | bytes 163840 | tf_op jit(solution)/shard_map/all_to_all | solution.py:95
  554.8 5.9 all-to-all-start.5
  560.8 6.4 pad_maximum_fusion
  569.0 4.8 all-to-all-start.4
  605.9 4.2 copy.407
  635.6 43.3 %all-to-all-done.4 = bf16[1,128,3,4,1536]{4,3,2,0,1:T(4,128)(2,1)} async-done(((bf16[1,128,3,4,1536]{4,3,2,0,1:T(4,128)(2,1)}), bf16[1,128,3,4,1536]{4,3,2,0,1:T(4,128)(2,1)}, u32[]{:S(2)}, u32[]{:S(2)}) %all-to-all-start.4) | async-done | bytes 4718624 | tf_op jit(solution)/shard_map/all_to_all | solution.py:93
  678.9 7.4 %convert_bitcast_fusion = f32[1,4,3,32,4,1536]{5,4,2,1,3,0:T(4,128)} fusion(bf16[1,32,4,3,4,1536]{5,4,3,2,1,0:T(4,128)(2,1)} %bitcast.133), kind=kLoop, calls=%fused_computation.3 | loop fusion | flops 2359296 | bytes 14155776 | tf_op jit(solution)/shard_map/convert_element_type | solution.py:121
  686.3 11.8 %copy.447 = f32[1,4,3,32,4,1536]{5,1,4,3,2,0:T(4,128)} copy(f32[1,4,3,32,4,1536]{5,4,2,1,3,0:T(4,128)} %convert_bitcast_fusion) | data formatting | bytes 18874368 | tf_op jit(solution)/shard_map/convert_element_type | solution.py:121
  698.1 12.0 %copy.454 = f32[1,4,3,128,1536]{3,4,2,1,0:T(8,128)} copy(f32[1,4,3,128,1536]{4,1,3,2,0:T(4,128)} %bitcast.266) | data formatting | bytes 18874368 | tf_op jit(solution)/shard_map/convert_element_type | solution.py:121
  710.1 8.8 %fusion.2 = bf16[1,4,3,128,1536]{3,4,2,1,0:T(8,128)(2,1)} fusion(f32[1,4,3,128,1536]{3,4,2,1,0:T(8,128)} %copy.454, f32[1,4,1,128,1536]{3,4,2,1,0:T(8,128)} %bitcast.278, f32[1,4,1,128,1536]{3,4,2,1,0:T(8,128)} %bitcast.277, f32[1,4,1,128,1536]{3,4,2,1,0:T(8,128)S(1)} %bitcast.276, f32[4,3,128,12]{2,3,0,1:T(8,128)S(1)} %get-tuple-element.6, ...), kind=kLoop, calls=%fused_computation.5 | loop fusion | flops 16515072 | bytes 23814144 | tf_op jit(solution)/shard_map/convert_element_type | solution.py:123
  718.9 6.6 copy.456
  (157 shorter events, 151.9 us)
Async XLA Ops:
  6.5 145.7 %all-gather.3.cloned.1.call-start = ((), (), s32[]{:S(2)}) async-start(), calls=%async_computation.6 | async-start | bytes 9732096 | tf_op jit(solution)/shard_map/all_gather | solution.py:57
  7.3 282.0 %all-gather.5.cloned.1.call-start = ((), (), s32[]{:S(2)}) async-start(), calls=%async_computation.7 | async-start | bytes 9732096 | tf_op jit(solution)/shard_map/all_gather | solution.py:56
  16.2 164.0 %all-to-all-start.2 = ((bf16[1,4,3,128,1536]{4,1,2,0,3:T(4,128)(2,1)}), bf16[1,4,3,128,1536]{4,1,2,0,3:T(4,128)(2,1)}, u32[]{:S(2)}, u32[]{:S(2)}) async-start(bf16[1,4,3,128,1536]{4,1,2,0,3:T(4,128)(2,1)} %copy.418), calls=%async_computation.2 | async-start | bytes 9437184 | tf_op jit(solution)/shard_map/all_to_all | solution.py:62
  180.2 144.1 %all-to-all-start = ((bf16[1,4,3,128,1536]{4,1,2,0,3:T(4,128)(2,1)}), bf16[1,4,3,128,1536]{4,1,2,0,3:T(4,128)(2,1)}, u32[]{:S(2)}, u32[]{:S(2)}) async-start(bf16[1,4,3,128,1536]{4,1,2,0,3:T(4,128)(2,1)} %copy.400), calls=%async_computation | async-start | bytes 9437184 | tf_op jit(solution)/shard_map/all_to_all | solution.py:64
  317.2 10.8 %copy-start.29 = (s32[1,4,3,2,2]{1,4,3,2,0:T(2,128)S(1)}, s32[1,4,3,2,2]{1,4,3,2,0:T(2,128)}, u32[]{:S(2)}) copy-start(s32[1,4,3,2,2]{1,4,3,2,0:T(2,128)} %param.9) | copy-start | bytes 580
  324.2 169.1 %all-to-all-start.1 = ((bf16[1,4,3,128,1536]{4,1,2,0,3:T(4,128)(2,1)}), bf16[1,4,3,128,1536]{4,1,2,0,3:T(4,128)(2,1)}, u32[]{:S(2)}, u32[]{:S(2)}) async-start(bf16[1,4,3,128,1536]{4,1,2,0,3:T(4,128)(2,1)} %copy.404), calls=%async_computation.1 | async-start | bytes 9437184 | tf_op jit(solution)/shard_map/all_to_all | solution.py:63
  442.8 5.0 copy-start.31
  519.5 35.3 %all-to-all-start.3 = ((f32[32,1,576]{2,1,0:T(1,128)}), f32[32,1,576]{2,1,0:T(1,128)S(1)}, u32[]{:S(2)}, u32[]{:S(2)}) async-start(f32[32,1,576]{2,1,0:T(1,128)} %reshape.1497), calls=%async_computation.3 | async-start | bytes 163840 | tf_op jit(solution)/shard_map/all_to_all | solution.py:95
  539.3 3.9 copy-start.3
  539.3 3.9 copy-start.17
  545.6 5.4 copy-start.24
  545.6 5.4 copy-start.25
  546.9 13.9 %copy-start.7 = (bf16[1,128,1,4,1536]{4,3,2,0,1:T(4,128)(2,1)S(1)}, bf16[1,128,1,4,1536]{4,3,2,0,1:T(4,128)(2,1)}, u32[]{:S(2)}) copy-start(bf16[1,128,1,4,1536]{4,3,2,0,1:T(4,128)(2,1)} %copy.444) | copy-start | bytes 4718596
  554.8 13.5 %all-to-all-start.5 = ((f32[32,1,576]{2,1,0:T(1,128)}), f32[32,1,576]{2,1,0:T(1,128)S(1)}, u32[]{:S(2)}, u32[]{:S(2)}) async-start(f32[32,1,576]{2,1,0:T(1,128)} %reshape.1495), calls=%async_computation.5 | async-start | bytes 163840 | tf_op jit(solution)/shard_map/all_to_all | solution.py:96
  569.0 109.9 %all-to-all-start.4 = ((bf16[1,128,3,4,1536]{4,3,2,0,1:T(4,128)(2,1)}), bf16[1,128,3,4,1536]{4,3,2,0,1:T(4,128)(2,1)}, u32[]{:S(2)}, u32[]{:S(2)}) async-start(bf16[1,128,3,4,1536]{4,3,2,0,1:T(4,128)(2,1)} %pad_maximum_fusion), calls=%async_computation.4 | async-start | bytes 9437184 | tf_op jit(solution)/shard_map/all_to_all | solution.py:93
  579.4 4.3 copy-start.30
  579.4 4.5 copy-start.32
  579.4 4.6 copy-start.5
  581.0 4.7 copy-start.4
  585.7 4.3 copy-start.6
  587.3 4.3 copy-start.10
  624.4 9.5 %copy-start.27 = (f32[4,128,12]{1,2,0:T(8,128)S(1)}, f32[4,128,12]{1,2,0:T(8,128)}, u32[]{:S(2)}) copy-start(f32[4,128,12]{1,2,0:T(8,128)} %fusion.8) | copy-start | bytes 73732
  624.4 9.5 %copy-start.28 = (f32[4,128,12]{1,2,0:T(8,128)S(1)}, f32[4,128,12]{1,2,0:T(8,128)}, u32[]{:S(2)}) copy-start(f32[4,128,12]{1,2,0:T(8,128)} %fusion.10) | copy-start | bytes 73732
  698.1 12.0 %copy-start.20 = (f32[4,3,128,12]{2,3,0,1:T(8,128)S(1)}, f32[4,3,128,12]{2,3,0,1:T(8,128)}, u32[]{:S(2)}) copy-start(f32[4,3,128,12]{2,3,0,1:T(8,128)} %get-tuple-element.7) | copy-start | bytes 221188
  (17 other events, 31.8 us)
Sparse Core Ops, SparseCore 0:
  10.2 141.9 all-gather.2
  155.2 134.0 all-gather.4
where the time goes:
time: 743 us; the launch traced here: 733 us
  waiting for transfers between devices  287 us (39%)
  local copies, waits for them, and re-layouts  173 us (23%)
  blocking collectives  114 us (15%)
  matrix products  64.8 us (9%)
  starting transfers between devices  45.5 us (6%)
  other arithmetic  34.7 us (5%)
  between operations  14.1 us (2%)
    all_gather x1, waiting for transfers between devices, on_device(): lax.all_gather(value_weight, 'seq', axis=0, tiled=True)  129 us
    all_gather x1, blocking collectives, on_device(): code_table = lax.all_gather(halves, 'seq', axis=1, tiled=True)  114 us
    all_gather x1, waiting for transfers between devices, on_device(): key_sum = add_panel(lax.all_gather(key_weight, 'seq', axis=0, tiled=True))  105 us
    all_to_all x1, waiting for transfers between devices, on_device(): lax.all_to_all(remote_mean, 'seq', split_axis=1, concat_axis=3, tiled=True)  43.3 us
    dot_general x2, matrix products, add_panel(): return jnp.dot(home_rows, weight_panel, preferred_element_type=jnp.float32)  39.8 us
    unnamed x78, local copies, waits for them, and re-layouts  39.1 us
    convert_element_type x2, local copies, waits for them, and re-layouts, on_device(): back_mean.astype(jnp.float32)  23.8 us
    all_to_all x1, starting transfers between devices, on_device(): lax.all_to_all(remote_peak, 'seq', split_axis=1, concat_axis=3, tiled=True)  19.8 us
  transfers between devices with their start and end apart: 8, of which 5 were waited for; matrix products, arithmetic and copies ran while one was open for 26% of the time, Pallas kernels for 0%

commit v1 on v0

--- a/solution.py
+++ b/solution.py
@@ -90,7 +90,12 @@
     remote_mean = remote_mean.reshape(remote_mean.shape[:4] + (hidden_width,)).astype(jnp.bfloat16)
     remote_peak = jnp.stack([result[1] for result in remote_results], axis=2)
     remote_sum = jnp.stack([result[2] for result in remote_results], axis=2)
-    back_mean = lax.all_to_all(remote_mean, "seq", split_axis=1, concat_axis=3, tiled=True)
+    back_mean = jnp.concatenate(
+        lax.all_to_all(
+            jnp.stack(jnp.split(remote_mean, lax.axis_size("seq"), axis=1)), "seq", 0, 0
+        ),
+        axis=3,
+    )
     back_peak, back_sum = (
         lax.all_to_all(remote_peak, "seq", split_axis=1, concat_axis=3, tiled=True),
         lax.all_to_all(remote_sum, "seq", split_axis=1, concat_axis=3, tiled=True),

time: 743 us -> 755 us (1.016)
  local copies, waits for them, and re-layouts: 173 us -> 186 us
    unnamed x78 -> x83, local copies, waits for them, and re-layouts: 39.1 us -> 45.5 us
  transfers between devices with their start and end apart: 8 -> 8, of which waited for: 5 -> 5; matrix products, arithmetic and copies ran while one was open for 26% -> 25% of each run, Pallas kernels for 0% -> 0%
where the time goes in v1:
time: 755 us; the launch traced here: 744 us
  waiting for transfers between devices  290 us (38%)
  local copies, waits for them, and re-layouts  186 us (25%)
  blocking collectives  114 us (15%)
  matrix products  66.7 us (9%)
  starting transfers between devices  43.9 us (6%)
  other arithmetic  29.5 us (4%)
  between operations  14.3 us (2%)
    all_gather x1, waiting for transfers between devices, on_device(): lax.all_gather(value_weight, 'seq', axis=0, tiled=True)  129 us
    all_gather x1, blocking collectives, on_device(): code_table = lax.all_gather(halves, 'seq', axis=1, tiled=True)  114 us
    all_gather x1, waiting for transfers between devices, on_device(): key_sum = add_panel(lax.all_gather(key_weight, 'seq', axis=0, tiled=True))  105 us
    unnamed x83, local copies, waits for them, and re-layouts  45.5 us
    all_to_all x1, waiting for transfers between devices, on_device(): lax.all_to_all(jnp.stack(jnp.split(remote_mean, lax.axis_size('seq'), axi...  41.5 us
    dot_general x2, matrix products, add_panel(): return jnp.dot(home_rows, weight_panel, preferred_element_type=jnp.float32)  39.8 us
    convert_element_type x2, local copies, waits for them, and re-layouts, on_device(): back_mean.astype(jnp.float32)  22.5 us
    all_to_all x1, starting transfers between devices, on_device(): lax.all_to_all(remote_peak, 'seq', split_axis=1, concat_axis=3, tiled=True)  19.6 us
  transfers between devices with their start and end apart: 8, of which 5 were waited for; matrix products, arithmetic and copies ran while one was open for 25% of the time, Pallas kernels for 0%

profile of v1, /device:TPU:0, one launch (start us, length us, event | category | flops | bytes accessed | tf_op | source)
XLA Modules:
  0.0 744.3 jit_solution(7172693686559763132)
XLA Ops:
  8.0 8.2 %copy.445 = bf16[1,4,3,128,1536]{4,1,2,0,3:T(4,128)(2,1)} copy(bf16[1,4,3,128,1536]{4,3,2,1,0:T(8,128)(2,1)} %param.6) | data formatting | bytes 9437184 | tf_op args[1]
  16.2 7.4 all-to-all-start.2
  23.6 128.6 %all-gather.3.cloned.1.call-done = bf16[3072,1536]{1,0:T(8,128)(2,1)} async-done(((bf16[96,1536]{1,0:T(8,128)(2,1)}), bf16[3072,1536]{1,0:T(8,128)(2,1)}) %all-gather.3.cloned.1.call-update) | async-done | bytes 9437200 | tf_op jit(solution)/shard_map/all_gather | solution.py:57
  152.2 19.9 %convolution_convert_fusion.1 = bf16[1536,1536]{1,0:T(8,128)(2,1)S(1)} fusion(bf16[1536,3072]{1,0:T(8,128)(2,1)} %bitcast.452, bf16[3072,1536]{1,0:T(8,128)(2,1)} %all-gather.3.cloned.1.call-done), kind=kOutput, calls=%fused_computation.7 | convolution fusion | flops 14497873920 | bytes 23592960 | tf_op jit(solution)/shard_map/dot_general | solution.py:54
  174.3 5.8 copy.427
  183.9 105.3 %all-gather.5.cloned.1.call-done = bf16[3072,1536]{1,0:T(8,128)(2,1)} async-done(((bf16[96,1536]{1,0:T(8,128)(2,1)}), bf16[3072,1536]{1,0:T(8,128)(2,1)}) %all-gather.5.cloned.1.call-update) | async-done | bytes 9437200 | tf_op jit(solution)/shard_map/all_gather | solution.py:56
  289.2 19.9 %convolution_convert_fusion = bf16[1536,1536]{1,0:T(8,128)(2,1)S(1)} fusion(bf16[1536,3072]{1,0:T(8,128)(2,1)} %bitcast.453, bf16[3072,1536]{1,0:T(8,128)(2,1)} %all-gather.5.cloned.1.call-done), kind=kOutput, calls=%fused_computation.6 | convolution fusion | flops 14497873920 | bytes 23592960 | tf_op jit(solution)/shard_map/dot_general | solution.py:54
  311.4 5.8 copy.431
  317.2 7.0 all-to-all-done
  328.0 113.8 %all_gather.11 = s32[1,128,3,2,2]{2,4,3,0,1:T(2,128)S(1)} all-gather(s32[1,4,3,2,2]{2,4,3,0,1:T(2,128)S(1)} %copy.442), channel_id=1, replica_groups=mesh['parts'=1,'seq'=32] {'seq'}, dimensions={1}, use_global_device_ids=true | all-gather | bytes 6336 | tf_op jit(solution)/shard_map/all_gather | solution.py:66
  443.1 4.7 copy.446
  466.4 4.6 fusion.128
  495.5 4.0 copy.467
  538.2 19.6 %all-to-all-start.3 = ((f32[32,1,576]{2,1,0:T(1,128)}), f32[32,1,576]{2,1,0:T(1,128)S(1)}, u32[]{:S(2)}, u32[]{:S(2)}) async-start(f32[32,1,576]{2,1,0:T(1,128)} %reshape.1496), calls=%async_computation.3 | async-start | bytes 163840 | tf_op jit(solution)/shard_map/all_to_all | solution.py:100
  568.9 5.8 all-to-all-start.5
  576.4 5.9 all-to-all-done.5
  586.5 4.6 fusion.127
  621.0 4.1 copy.434
  650.2 41.5 %all-to-all-done.4 = bf16[32,1,4,3,4,1536]{5,2,4,3,1,0:T(4,128)(2,1)} async-done(((bf16[32,1,4,3,4,1536]{5,2,4,3,1,0:T(4,128)(2,1)}), bf16[32,1,4,3,4,1536]{5,2,4,3,1,0:T(4,128)(2,1)}, u32[]{:S(2)}, u32[]{:S(2)}) %all-to-all-start.4) | async-done | bytes 4718624 | tf_op jit(solution)/shard_map/all_to_all | solution.py:94
  691.7 7.5 %convert_bitcast_fusion = f32[1,4,3,32,4,1536]{5,1,4,2,0,3:T(4,128)} fusion(bf16[32,1,4,3,4,1536]{5,2,4,3,1,0:T(4,128)(2,1)} %all-to-all-done.4), kind=kLoop, calls=%fused_computation.4 | loop fusion | flops 2359296 | bytes 14155776 | tf_op jit(solution)/shard_map/convert_element_type | solution.py:126
  699.1 10.4 %copy.474 = f32[1,4,3,32,4,1536]{5,1,4,3,2,0:T(4,128)} copy(f32[1,4,3,32,4,1536]{5,1,4,2,0,3:T(4,128)} %convert_bitcast_fusion) | data formatting | bytes 18874368 | tf_op jit(solution)/shard_map/convert_element_type | solution.py:126
  709.6 12.0 %copy.481 = f32[1,4,3,128,1536]{3,4,2,1,0:T(8,128)} copy(f32[1,4,3,128,1536]{4,1,3,2,0:T(4,128)} %bitcast.392) | data formatting | bytes 18874368 | tf_op jit(solution)/shard_map/convert_element_type | solution.py:126
  721.6 8.8 %fusion.2 = bf16[1,4,3,128,1536]{3,4,2,1,0:T(8,128)(2,1)} fusion(f32[1,4,3,128,1536]{3,4,2,1,0:T(8,128)} %copy.481, f32[1,4,1,128,1536]{3,4,2,1,0:T(8,128)} %bitcast.404, f32[1,4,1,128,1536]{3,4,2,1,0:T(8,128)} %bitcast.403, f32[1,4,1,128,1536]{3,4,2,1,0:T(8,128)S(1)} %bitcast.402, f32[4,3,128,12]{2,3,0,1:T(8,128)S(1)} %get-tuple-element.6, ...), kind=kLoop, calls=%fused_computation.5 | loop fusion | flops 16515072 | bytes 23814144 | tf_op jit(solution)/shard_map/convert_element_type | solution.py:128
  730.4 6.6 copy.483
  (163 shorter events, 168.0 us)
Async XLA Ops:
  6.5 145.7 %all-gather.3.cloned.1.call-start = ((), (), s32[]{:S(2)}) async-start(), calls=%async_computation.6 | async-start | bytes 9732096 | tf_op jit(solution)/shard_map/all_gather | solution.py:57
  7.3 282.0 %all-gather.5.cloned.1.call-start = ((), (), s32[]{:S(2)}) async-start(), calls=%async_computation.7 | async-start | bytes 9732096 | tf_op jit(solution)/shard_map/all_gather | solution.py:56
  16.2 164.0 %all-to-all-start.2 = ((bf16[1,4,3,128,1536]{4,1,2,0,3:T(4,128)(2,1)}), bf16[1,4,3,128,1536]{4,1,2,0,3:T(4,128)(2,1)}, u32[]{:S(2)}, u32[]{:S(2)}) async-start(bf16[1,4,3,128,1536]{4,1,2,0,3:T(4,128)(2,1)} %copy.445), calls=%async_computation.2 | async-start | bytes 9437184 | tf_op jit(solution)/shard_map/all_to_all | solution.py:62
  172.2 2.1 copy-start.1
  180.1 144.1 %all-to-all-start = ((bf16[1,4,3,128,1536]{4,1,2,0,3:T(4,128)(2,1)}), bf16[1,4,3,128,1536]{4,1,2,0,3:T(4,128)(2,1)}, u32[]{:S(2)}, u32[]{:S(2)}) async-start(bf16[1,4,3,128,1536]{4,1,2,0,3:T(4,128)(2,1)} %copy.427), calls=%async_computation | async-start | bytes 9437184 | tf_op jit(solution)/shard_map/all_to_all | solution.py:64
  309.2 2.2 copy-start.2
  317.2 10.7 %copy-start.19 = (s32[1,4,3,2,2]{1,4,3,2,0:T(2,128)S(1)}, s32[1,4,3,2,2]{1,4,3,2,0:T(2,128)}, u32[]{:S(2)}) copy-start(s32[1,4,3,2,2]{1,4,3,2,0:T(2,128)} %param.9) | copy-start | bytes 580
  324.2 175.4 %all-to-all-start.1 = ((bf16[1,4,3,128,1536]{4,1,2,0,3:T(4,128)(2,1)}), bf16[1,4,3,128,1536]{4,1,2,0,3:T(4,128)(2,1)}, u32[]{:S(2)}, u32[]{:S(2)}) async-start(bf16[1,4,3,128,1536]{4,1,2,0,3:T(4,128)(2,1)} %copy.431), calls=%async_computation.1 | async-start | bytes 9437184 | tf_op jit(solution)/shard_map/all_to_all | solution.py:63
  476.3 1.4 copy-start.13
  538.2 30.7 %all-to-all-start.3 = ((f32[32,1,576]{2,1,0:T(1,128)}), f32[32,1,576]{2,1,0:T(1,128)S(1)}, u32[]{:S(2)}, u32[]{:S(2)}) async-start(f32[32,1,576]{2,1,0:T(1,128)} %reshape.1496), calls=%async_computation.3 | async-start | bytes 163840 | tf_op jit(solution)/shard_map/all_to_all | solution.py:100
  560.4 2.4 copy-start
  562.8 2.2 copy-start.10
  568.9 13.4 %all-to-all-start.5 = ((f32[32,1,576]{2,1,0:T(1,128)}), f32[32,1,576]{2,1,0:T(1,128)S(1)}, u32[]{:S(2)}, u32[]{:S(2)}) async-start(f32[32,1,576]{2,1,0:T(1,128)} %reshape.1494), calls=%async_computation.5 | async-start | bytes 163840 | tf_op jit(solution)/shard_map/all_to_all | solution.py:101
  582.9 108.7 %all-to-all-start.4 = ((bf16[32,1,4,3,4,1536]{5,2,4,3,1,0:T(4,128)(2,1)}), bf16[32,1,4,3,4,1536]{5,2,4,3,1,0:T(4,128)(2,1)}, u32[]{:S(2)}, u32[]{:S(2)}) async-start(bf16[32,1,4,3,4,1536]{5,2,4,3,1,0:T(4,128)(2,1)} %fusion.63), calls=%async_computation.4 | async-start | bytes 9437184 | tf_op jit(solution)/shard_map/all_to_all | solution.py:94
  600.8 4.3 copy-start.3
  602.4 4.3 copy-start.5
  608.9 1.4 copy-start.4
  608.9 1.9 copy-start.6
  611.6 1.5 copy-start.8
  627.8 1.5 copy-start.9
  629.2 3.2 copy-start.16
  639.2 9.4 %copy-start.17 = (f32[4,128,12]{1,2,0:T(8,128)S(1)}, f32[4,128,12]{1,2,0:T(8,128)}, u32[]{:S(2)}) copy-start(f32[4,128,12]{1,2,0:T(8,128)} %fusion.8) | copy-start | bytes 73732
  639.2 9.4 %copy-start.18 = (f32[4,128,12]{1,2,0:T(8,128)S(1)}, f32[4,128,12]{1,2,0:T(8,128)}, u32[]{:S(2)}) copy-start(f32[4,128,12]{1,2,0:T(8,128)} %fusion.10) | copy-start | bytes 73732
  709.6 12.0 %copy-start.14 = (f32[4,3,128,12]{2,3,0,1:T(8,128)S(1)}, f32[4,3,128,12]{2,3,0,1:T(8,128)}, u32[]{:S(2)}) copy-start(f32[4,3,128,12]{2,3,0,1:T(8,128)} %get-tuple-element.7) | copy-start | bytes 221188
  (4 other events, 4.9 us)
Sparse Core Ops, SparseCore 0:
  10.2 141.9 all-gather.2
  155.1 134.0 all-gather.4
